TPU v7x, 32 devices: a whole 2x2x4 slice. The times are simulated.
32 devices in a mesh: grp: 4 (over y, core), row: 8 (over z, x).
Axes of the slice: x: 2, y: 2, z: 4, core: 2. Of those that a mesh axis runs over, the one named last changes fastest.
Arguments:
- grad: float32 [32, 2048, 512], P('grp', 'row')
- weight: bfloat16 [32, 2048, 512], P('grp', 'row'), may hold values from -0.125 to 0.125
- owner: int32 [32, 1], P('grp'), may hold values from 0 to 7; in each aligned block of 8 rows (0 to 7, 8 to 15, ...) at most 2 rows name the same one
- tokens: bfloat16 [3072, 2048], P('row'), may hold values from -6 to 6
- counts: int32 [8], P('row'), may hold values from 96 to 384, as said below
Outputs:
- new_weight: bfloat16 [32, 2048, 512], P('grp', 'row')
- mixed: bfloat16 [3072, 512], P('row', 'grp')
Inputs may be any that keep to these rules, and one draw needn't show every extreme that they name: Within each group's 8 consecutive matrices no owner is named more than 2 times, a bound that some block reaches. `counts`: some row index has all 384 rows live.
All inputs are finite; a program needn't handle non-finite values.
Results may differ from a plain program's by a relative error of at most 0.017.
Values may be sent and summed in bfloat16 or wider, within the bound.
A program may use at most 128 MiB of HBM per device.

v0:
```python
import functools

import jax
import jax.numpy as jnp
from jax import lax
from jax.experimental import pallas as pl
from jax.experimental.pallas import tpu as pltpu
from jax.sharding import PartitionSpec as P

ITERS = 5
MOST = 2
CORES = 2
LAGS = (1, 3)

coef_a = 3.4445
coef_b = -4.775
coef_c = 2.0315
step_size = 0.5

f32 = jnp.float32
bf16 = jnp.bfloat16
MESH = pl.DeviceIdType.MESH


def far_first(n):
    return sorted(range(1, n), key=lambda k: abs(k - n // 2))


def greet(n, groups, grp_shifts):
    row, grp = lax.axis_index("row"), lax.axis_index("grp")
    barrier = pltpu.get_barrier_semaphore()
    for k in range(1, n):
        pl.semaphore_signal(
            barrier, inc=1, device_id=(grp, lax.rem(row + k, n)), device_id_type=MESH
        )
    for g in grp_shifts:
        pl.semaphore_signal(barrier, inc=1, device_id=(g, row), device_id_type=MESH)
    pl.semaphore_wait(barrier, n - 1 + len(grp_shifts))


def ortho_kernel(
    n, groups, raw, tokens, back, cols, x, acc, gram, poly, ssem, rsem, tss, trs, gss, grs, bss, brs, own_sem
):
    row, grp = lax.axis_index("row"), lax.axis_index("grp")
    width = raw.shape[2]
    others = [lax.rem(grp + k, groups) for k in range(1, groups)]
    greet(n, groups, others)
    order = far_first(n)

    def remote(src, dst, ss, rs, where):
        return pltpu.make_async_remote_copy(
            src_ref=src, dst_ref=dst, send_sem=ss, recv_sem=rs, device_id=where, device_id_type=MESH
        )

    def share_of(to):
        size, wide = cols.shape[2], cols.shape[3]
        down = pl.ds(pl.multiple_of(grp * size, size), size)
        return tokens.at[down, pl.ds(pl.multiple_of(to * wide, wide), wide)]

    sends, tsends = {}, {}
    for k in order:
        to = lax.rem(row + k, n)
        sends[k] = remote(raw.at[to], x.at[row], ssem.at[k], rsem.at[k], (grp, to))
        sends[k].start()
    for k in order:
        to = lax.rem(row + k, n)
        tsends[k] = remote(share_of(to), cols.at[grp, row], tss.at[k], trs.at[k], (grp, to))
        tsends[k].start()

    def self_dot(v):
        return lax.dot_general(v, v, (((0,), (0,)), ((), ())), preferred_element_type=f32)

    x[row] = raw[row]
    own = pltpu.make_async_copy(share_of(row), cols.at[grp, row], own_sem)
    own.start()
    acc[...] = self_dot(raw[row])
    for k in reversed(order):
        sends[k].wait_recv()
        acc[...] += self_dot(x[lax.rem(row + n - k, n)])

    total = acc[...]
    eye = lax.broadcasted_iota(jnp.int32, total.shape, 0) == lax.broadcasted_iota(
        jnp.int32, total.shape, 1
    )
    norm2 = jnp.sum(jnp.where(eye, total, 0.0), keepdims=True)
    scale = 1.0 / (jnp.sqrt(norm2) + 1e-07)
    acc[...] = jnp.where(norm2 < jnp.inf, scale * (scale * total), 0.0)

    gsends = []
    for turn in range(ITERS):
        first, last = turn == 0, turn == ITERS - 1
        gram[...] = acc[...].astype(bf16)
        square = jnp.dot(gram[...], gram[...], preferred_element_type=f32)
        poly[...] = (coef_b * gram[...].astype(f32) + coef_c * square).astype(bf16)

        def fresh(i):
            block = x[i]
            update = jnp.dot(block, poly[...], preferred_element_type=f32)
            if first:
                return ((coef_a * scale) * block.astype(f32) + scale * update).astype(bf16)
            return (coef_a * block.astype(f32) + update).astype(bf16)

        if not last:
            acc[...] = jnp.zeros_like(acc)

            def step(i, carry):
                block = fresh(i)
                x[i] = block
                acc[...] += self_dot(block)
                return carry

            lax.fori_loop(0, n, step, 0)
        if first:
            own.wait()
            for k in order:
                tsends[k].wait_recv()
            for j, g in enumerate(others):
                copy = remote(cols.at[grp], cols.at[grp], gss.at[j], grs.at[j], (g, row))
                copy.start()
                gsends.append(copy)
        if last:
            bsends = {}
            for k in order:
                to = lax.rem(row + k, n)
                x[to] = fresh(to)
                bsends[k] = remote(x.at[to], back.at[row], bss.at[k], brs.at[k], (grp, to))
                bsends[k].start()
            back[row] = fresh(row)
    for k in order:
        sends[k].wait_send()
        tsends[k].wait_send()
    for copy in gsends:
        copy.wait()
    for k in order:
        bsends[k].wait()


def project_kernel(
    n, groups, index, valid, cols, fresh, out, part, got1, sum1, got2, sum2, got3,
    ss1, rs1, ss2, rs2, ss3, rs3
):
    row, grp = lax.axis_index("row"), lax.axis_index("grp")
    ys = groups // CORES
    y, core = grp // CORES, lax.rem(grp, CORES)
    count, piece = out.shape
    partners = [y * CORES + (1 - core)]
    partners += [lax.rem(y + j, ys) * CORES + core for j in range(1, ys)]
    greet(n, groups, partners)
    order = far_first(n) + [0]

    def remote(src, dst, ss, rs, where):
        copy = pltpu.make_async_remote_copy(
            src_ref=src, dst_ref=dst, send_sem=ss, recv_sem=rs, device_id=where, device_id_type=MESH
        )
        copy.start()
        return copy

    one, two, three = {}, {}, {}

    def stage1(k):
        b = lax.rem(row + k, n)
        tok = cols[:, b].reshape(count, cols.shape[3])
        total = jnp.zeros((count, groups * piece), f32)
        for s in range(MOST):
            term = jnp.dot(tok, fresh[index[b, s]], preferred_element_type=f32)
            total = total + jnp.where(valid[b, s] > 0, term, 0.0)
        total = (total * groups ** (-0.5)).astype(bf16)
        for g in range(groups):
            part[k, g % CORES, g // CORES] = total[:, g * piece : (g + 1) * piece]
        one[k] = remote(part.at[k, 1 - core], got1.at[k], ss1.at[k], rs1.at[k], (partners[0], row))

    def stage2(k):
        one[k].wait_recv()
        two[k] = []
        for j in range(1, ys):
            to = lax.rem(y + j, ys)
            both = part[k, core, to].astype(f32) + got1[k, to].astype(f32)
            sum1[k, j] = both.astype(bf16)
            two[k].append(
                remote(sum1.at[k, j], got2.at[k, j], ss2.at[k, j], rs2.at[k, j], (partners[j], row))
            )

    def stage3(k):
        total = part[k, core, y].astype(f32) + got1[k, y].astype(f32)
        for j in range(1, ys):
            two[k][j - 1].wait_recv()
            total = total + got2[k, j].astype(f32)
        if k == 0:
            return total
        sum2[k] = total.astype(bf16)
        to = lax.rem(row + k, n)
        three[k] = remote(sum2.at[k], got3.at[k], ss3.at[k], rs3.at[k], (grp, to))

    final = None
    lag2, lag3 = LAGS
    for i in range(n + lag3):
        if i < n:
            stage1(order[i])
        if lag2 <= i < n + lag2:
            stage2(order[i - lag2])
        if lag3 <= i < n + lag3:
            final = stage3(order[i - lag3])
    for k in reversed(order[:-1]):
        three[k].wait_recv()
        final = final + got3[k].astype(f32)
    out[...] = final.astype(bf16)
    for k in order:
        one[k].wait_send()
        for copy in two[k]:
            copy.wait_send()
        if k:
            three[k].wait_send()


VM = pl.BlockSpec(memory_space=pltpu.VMEM)
SM = pl.BlockSpec(memory_space=pltpu.SMEM)


def body(grad, weight, owner, tokens, counts):
    ranks = lax.axis_size("row")
    groups = lax.axis_size("grp")
    number, rows, width = grad.shape
    assert number == ranks
    ys = groups // CORES
    dma = pltpu.SemaphoreType.DMA
    top = float(jnp.finfo(bf16).max)
    raw = jnp.clip(grad, -top, top).astype(bf16)

    count = tokens.shape[0]
    share = count // groups
    back, cols = pl.pallas_call(
        functools.partial(ortho_kernel, ranks, groups),
        out_shape=[
            jax.ShapeDtypeStruct((ranks, rows, width), bf16),
            jax.ShapeDtypeStruct((groups, ranks, share, rows), bf16),
        ],
        in_specs=[VM, pl.BlockSpec(memory_space=pl.ANY)],
        out_specs=[VM, VM],
        scratch_shapes=[
            pltpu.VMEM((ranks, rows, width), bf16),
            pltpu.VMEM((width, width), f32),
            pltpu.VMEM((width, width), bf16),
            pltpu.VMEM((width, width), bf16),
        ]
        + [dma((ranks,))] * 4
        + [dma((groups,))] * 2
        + [dma((ranks,))] * 2
        + [dma],
        compiler_params=pltpu.CompilerParams(
            collective_id=0, has_side_effects=True, vmem_limit_bytes=48 * 1024 * 1024
        ),
        name="ortho",
    )(raw, tokens)
    new_weight = (weight.astype(f32) - step_size * back.astype(f32)).astype(bf16)

    target = owner[:, 0]
    before = jnp.arange(number)[None, :] < jnp.arange(number)[:, None]
    same = target[None, :] == target[:, None]
    slot = jnp.sum((same & before).astype(jnp.int32), axis=1)
    hit = (target[None, None, :] == jnp.arange(ranks)[:, None, None]) & (
        slot[None, None, :] == jnp.arange(MOST)[None, :, None]
    )
    index = jnp.sum(hit * jnp.arange(number)[None, None, :], axis=2).astype(jnp.int32)
    valid = jnp.any(hit, axis=2).astype(jnp.int32)

    piece = width // groups
    summed = pl.pallas_call(
        functools.partial(project_kernel, ranks, groups),
        out_shape=jax.ShapeDtypeStruct((count, piece), bf16),
        in_specs=[SM, SM, VM, VM],
        out_specs=VM,
        scratch_shapes=[
            pltpu.VMEM((ranks, CORES, ys, count, piece), bf16),
            pltpu.VMEM((ranks, ys, count, piece), bf16),
            pltpu.VMEM((ranks, ys, count, piece), bf16),
            pltpu.VMEM((ranks, ys, count, piece), bf16),
            pltpu.VMEM((ranks, count, piece), bf16),
            pltpu.VMEM((ranks, count, piece), bf16),
            dma((ranks,)),
            dma((ranks,)),
            dma((ranks, ys)),
            dma((ranks, ys)),
            dma((ranks,)),
            dma((ranks,)),
        ],
        compiler_params=pltpu.CompilerParams(
            collective_id=1, has_side_effects=True, vmem_limit_bytes=48 * 1024 * 1024
        ),
        name="project",
    )(index, valid, cols, new_weight)
    live = jnp.arange(count)[:, None] < counts[0]
    mixed = jnp.where(live, summed, jnp.zeros_like(summed))
    return (new_weight, mixed)


def solution(mesh):
    placed = (
        P("grp", "row", None),
        P("grp", "row", None),
        P("grp", None),
        P("row", None),
        P("row"),
    )
    return jax.shard_map(
        body,
        mesh=mesh,
        in_specs=placed,
        out_specs=(P("grp", "row", None), P("row", "grp")),
        check_vma=False,
    )
```

profile of v0, /device:TPU:0, one launch (start us, length us, event | category | flops | bytes accessed | tf_op | source)
XLA Modules:
  0.0 163.2 jit_solution(2354201790703311650)
XLA Ops:
  0.6 0.0 copy-start.1
  0.6 3.9 %clamp_convert_fusion.raw = bf16[8,256,512]{2,1,0:T(8,128)(2,1)} fusion(f32[8,256,512]{2,1,0:T(8,128)} %param.5), kind=kLoop, calls=%fused_computation.1 | loop fusion | flops 1048576 | bytes 6291456 | tf_op jit(solution)/shard_map/convert_element_type | solution.py:227
  4.5 0.0 copy-done.1
  4.5 0.0 copy-start.4
  4.5 115.3 %ortho.1 = (bf16[8,256,512]{2,1,0:T(8,128)(2,1)S(1)}, bf16[4,8,96,256]{3,2,1,0:T(8,128)(2,1)S(1)}) custom-call(bf16[8,256,512]{2,1,0:T(8,128)(2,1)} %clamp_convert_fusion.raw, bf16[384,2048]{1,0:T(8,128)(2,1)S(1)} %copy-done.1), custom_call_target="tpu_custom_call" | custom-call | tf_op jit(solution)/shard_map/ortho/pallas_call | solution.py:231
  119.8 0.0 copy-start.2
  119.8 0.0 copy-done.4
  119.8 0.0 copy-start.5
  119.9 0.7 subtract_convert_fusion.fresh
  120.5 0.6 copy-done.2
  121.1 0.0 copy-start
  121.1 0.0 copy-done.5
  121.1 0.2 convert_reduce_fusion
  121.3 0.1 fusion
  121.5 0.1 copy.8.index
  121.6 0.2 and_reduce_fusion
  121.7 0.1 copy.7
  121.8 0.0 copy-start.3
  121.8 1.4 copy-done.3
  123.2 38.5 %project.1 = bf16[384,128]{1,0:T(8,128)(2,1)S(1)} custom-call(s32[8,2]{1,0:T(8,128)S(1)} %copy.8.index, s32[8,2]{1,0:T(8,128)S(1)} %convert_element_type.24.valid, bf16[4,8,96,256]{3,2,1,0:T(8,128)(2,1)S(1)} %copy-done.3, bf16[8,256,512]{2,1,0:T(8,128)(2,1)S(1)} %subtract_convert_fusion.fresh), custom_call_target="tpu_custom_call" | custom-call | tf_op jit(solution)/shard_map/project/pallas_call | solution.py:267
  162.4 0.8 broadcast_select_fusion
  163.2 0.0 copy-done
  (4 shorter events, 0.0 us)
Async XLA Ops:
  0.6 3.9 %copy-start.1 = (bf16[384,2048]{1,0:T(8,128)(2,1)S(1)}, bf16[384,2048]{1,0:T(8,128)(2,1)}, u32[]{:S(2)}) copy-start(bf16[384,2048]{1,0:T(8,128)(2,1)} %tokens.1) | copy-start | bytes 4718596
  4.5 115.3 %copy-start.4 = (bf16[8,256,512]{2,1,0:T(8,128)(2,1)S(1)}, bf16[8,256,512]{2,1,0:T(8,128)(2,1)}, u32[]{:S(2)}) copy-start(bf16[8,256,512]{2,1,0:T(8,128)(2,1)} %param.6) | copy-start | bytes 6291460
  119.8 1.3 copy-start.2
  119.8 1.3 copy-start.5
  121.1 42.1 %copy-start = (bf16[8,256,512]{2,1,0:T(8,128)(2,1)}, bf16[8,256,512]{2,1,0:T(8,128)(2,1)S(1)}, u32[]{:S(2)}) copy-start(bf16[8,256,512]{2,1,0:T(8,128)(2,1)S(1)} %subtract_convert_fusion.fresh) | copy-start | bytes 6291460
  121.8 1.4 copy-start.3
where the time goes:
time: 163 us
  Pallas kernels  154 us (94%)
  other arithmetic  5.79 us (4%)
  local copies, waits for them, and re-layouts  2.23 us (1%)
    pallas_call x1, Pallas kernels, body(): pl.pallas_call(functools.partial(ortho_kernel, ranks, groups), out_shape=...  115 us
    pallas_call x1, Pallas kernels, body(): pl.pallas_call(functools.partial(project_kernel, ranks, groups), out_shap...  38.5 us
    convert_element_type x1, other arithmetic, body(): raw = jnp.clip(grad, -top, top).astype(bf16)  3.86 us

commit v1 on v0

--- a/solution.py
+++ b/solution.py
@@ -11,6 +11,7 @@
 MOST = 2
 CORES = 2
 LAGS = (1, 3)
+TILE = 128
 
 coef_a = 3.4445
 coef_b = -4.775
@@ -38,100 +39,220 @@
     pl.semaphore_wait(barrier, n - 1 + len(grp_shifts))
 
 
+def split(v):
+    high = v.astype(bf16)
+    return high, (v - high.astype(f32)).astype(bf16)
+
+
+def dot(a, b):
+    return jnp.dot(a, b, preferred_element_type=f32)
+
+
+def dot_t(a, b):
+    return lax.dot_general(a, b, (((0,), (0,)), ((), ())), preferred_element_type=f32)
+
+
+def iotas(size):
+    shape = (size, size)
+    return lax.broadcasted_iota(jnp.int32, shape, 0), lax.broadcasted_iota(jnp.int32, shape, 1)
+
+
+def block(i):
+    return slice(i * TILE, (i + 1) * TILE)
+
+
+def packed_rows(width):
+    count = width // TILE
+    return (count * (count - 1) // 2 + count // 2) * TILE + count // 2 * 8
+
+
+def pack(full, out):
+    count = full.shape[0] // TILE
+    row, col = iotas(TILE)
+    at = 0
+    for i in range(count):
+        for j in range(i + 1, count):
+            out[at : at + TILE] = full[block(i), block(j)]
+            at += TILE
+    for i in range(0, count, 2):
+        one, two = full[block(i), block(i)], full[block(i + 1), block(i + 1)]
+        out[at : at + TILE] = jnp.where(row <= col, one, two)
+        at += TILE
+        diagonal = jnp.sum(jnp.where(row == col, two, 0.0), axis=0, keepdims=True)
+        out[at : at + 8] = jnp.broadcast_to(diagonal, (8, TILE))
+        at += 8
+
+
+def unpack(packed, put):
+    count = 1
+    while packed_rows(count * TILE) < packed.shape[0]:
+        count += 1
+    row, col = iotas(TILE)
+    at = 0
+    for i in range(count):
+        for j in range(i + 1, count):
+            value = packed[at : at + TILE]
+            put(i, j, value)
+            put(j, i, value.T)
+            at += TILE
+    for i in range(0, count, 2):
+        both = packed[at : at + TILE]
+        turned = both.T
+        at += TILE
+        diagonal = jnp.broadcast_to(packed[at : at + 1], (TILE, TILE))
+        at += 8
+        put(i, i, jnp.where(row <= col, both, turned))
+        put(i + 1, i + 1, jnp.where(row > col, both, jnp.where(row < col, turned, diagonal)))
+
+
 def ortho_kernel(
-    n, groups, raw, tokens, back, cols, x, acc, gram, poly, ssem, rsem, tss, trs, gss, grs, bss, brs, own_sem
+    n, groups, grad, tokens, back, cols, stage, raw, afar, near, acc, full, gout, gin, qout, qin,
+    gh, gl, ph, qh, ql, th, tl,
+    lsem, fss, frs, nss, nrs, css, crs, dss, drs, ass, ars, bss, brs, tss, trs, gss, grs, own_sem
 ):
     row, grp = lax.axis_index("row"), lax.axis_index("grp")
-    width = raw.shape[2]
     others = [lax.rem(grp + k, groups) for k in range(1, groups)]
     greet(n, groups, others)
     order = far_first(n)
+    half = n // 2
+    side, seat = row // half, lax.rem(row, half)
+    mate = lax.rem(row + half, n)
+    near_order = far_first(half)
+    top = float(jnp.finfo(bf16).max)
+
+    def peer(k):
+        return side * half + lax.rem(seat + k, half)
+
+    def source(k):
+        return lax.rem(seat + half - k, half)
+
+    def across(r):
+        return lax.rem(r + half, n)
 
     def remote(src, dst, ss, rs, where):
-        return pltpu.make_async_remote_copy(
+        copy = pltpu.make_async_remote_copy(
             src_ref=src, dst_ref=dst, send_sem=ss, recv_sem=rs, device_id=where, device_id_type=MESH
         )
+        copy.start()
+        return copy
 
     def share_of(to):
         size, wide = cols.shape[2], cols.shape[3]
         down = pl.ds(pl.multiple_of(grp * size, size), size)
         return tokens.at[down, pl.ds(pl.multiple_of(to * wide, wide), wide)]
 
-    sends, tsends = {}, {}
-    for k in order:
-        to = lax.rem(row + k, n)
-        sends[k] = remote(raw.at[to], x.at[row], ssem.at[k], rsem.at[k], (grp, to))
-        sends[k].start()
+    plan = [(k, True) for k in near_order] + [(0, True)] + [(k, False) for k in near_order] + [(0, False)]
+    loads = []
+    for slot, (k, helping) in enumerate(plan):
+        index = across(peer(k)) if helping else peer(k)
+        load = pltpu.make_async_copy(grad.at[index], stage.at[slot], lsem.at[slot])
+        load.start()
+        loads.append((index, load))
+    fsends, nsends = {}, {}
+    for slot, (k, helping) in enumerate(plan):
+        index, load = loads[slot]
+        load.wait()
+        value = jnp.clip(stage[slot], -top, top).astype(bf16)
+        if k == 0:
+            (afar if helping else near)[seat] = value
+            continue
+        raw[slot] = value
+        if helping:
+            fsends[k] = remote(raw.at[slot], afar.at[seat], fss.at[k], frs.at[k], (grp, peer(k)))
+        else:
+            nsends[k] = remote(raw.at[slot], near.at[seat], nss.at[k], nrs.at[k], (grp, peer(k)))
+
+    acc[...] = dot_t(afar[seat], afar[seat])
+    for k in near_order:
+        fsends[k].wait_recv()
+        acc[...] += dot_t(afar[source(k)], afar[source(k)])
+    pack(acc, gout)
+    cross = remote(gout, gin, css, crs, (grp, mate))
+
+    tsends = {}
     for k in order:
         to = lax.rem(row + k, n)
         tsends[k] = remote(share_of(to), cols.at[grp, row], tss.at[k], trs.at[k], (grp, to))
-        tsends[k].start()
-
-    def self_dot(v):
-        return lax.dot_general(v, v, (((0,), (0,)), ((), ())), preferred_element_type=f32)
-
-    x[row] = raw[row]
     own = pltpu.make_async_copy(share_of(row), cols.at[grp, row], own_sem)
     own.start()
-    acc[...] = self_dot(raw[row])
-    for k in reversed(order):
-        sends[k].wait_recv()
-        acc[...] += self_dot(x[lax.rem(row + n - k, n)])
+
+    full[...] = dot_t(near[seat], near[seat])
+    for k in near_order:
+        nsends[k].wait_recv()
+        full[...] += dot_t(near[source(k)], near[source(k)])
+    cross.wait_recv()
+
+    def put_sum(i, j, value):
+        acc[block(i), block(j)] = value
+
+    pack(full, qout)
+    qout[...] = qout[...] + gin[...]
+    unpack(qout, put_sum)
 
     total = acc[...]
-    eye = lax.broadcasted_iota(jnp.int32, total.shape, 0) == lax.broadcasted_iota(
-        jnp.int32, total.shape, 1
-    )
+    down, right = iotas(total.shape[0])
+    eye = down == right
     norm2 = jnp.sum(jnp.where(eye, total, 0.0), keepdims=True)
     scale = 1.0 / (jnp.sqrt(norm2) + 1e-07)
-    acc[...] = jnp.where(norm2 < jnp.inf, scale * (scale * total), 0.0)
-
+    gh[...], gl[...] = split(jnp.where(norm2 < jnp.inf, scale * (scale * total), 0.0))
+
+    def whole(high, low):
+        return high[...].astype(f32) + low[...].astype(f32)
+
+    for turn in range(ITERS):
+        ph[...] = (coef_b * gh[...].astype(f32) + coef_c * dot(gh[...], gh[...])).astype(bf16)
+        if turn == 0:
+            factor = jnp.where(eye, coef_a, 0.0) + ph[...].astype(f32)
+        else:
+            factor = coef_a * whole(qh, ql) + (dot(qh[...], ph[...]) + dot(ql[...], ph[...]))
+        if turn < ITERS - 1:
+            qh[...], ql[...] = split(factor)
+            th[...], tl[...] = split(coef_a * whole(gh, gl) + (dot(gh[...], ph[...]) + dot(gl[...], ph[...])))
+            gh[...], gl[...] = split(coef_a * whole(th, tl) + (dot_t(ph[...], th[...]) + dot_t(ph[...], tl[...])))
+        else:
+            full[...] = scale * factor
+    pack(full, qout)
+    recross = remote(qout, qin, dss, drs, (grp, mate))
+    qh[...], ql[...] = split(full[...])
+
+    def apply(value):
+        return (dot(value, qh[...]) + dot(value, ql[...])).astype(bf16)
+
+    asends, bsends = {}, {}
+    for k in near_order:
+        at = lax.rem(seat + k, half)
+        near[at] = apply(near[at])
+        asends[k] = remote(near.at[at], back.at[row], ass.at[k], ars.at[k], (grp, peer(k)))
+    back[row] = apply(near[seat])
+
+    own.wait()
+    for k in order:
+        tsends[k].wait_recv()
     gsends = []
-    for turn in range(ITERS):
-        first, last = turn == 0, turn == ITERS - 1
-        gram[...] = acc[...].astype(bf16)
-        square = jnp.dot(gram[...], gram[...], preferred_element_type=f32)
-        poly[...] = (coef_b * gram[...].astype(f32) + coef_c * square).astype(bf16)
-
-        def fresh(i):
-            block = x[i]
-            update = jnp.dot(block, poly[...], preferred_element_type=f32)
-            if first:
-                return ((coef_a * scale) * block.astype(f32) + scale * update).astype(bf16)
-            return (coef_a * block.astype(f32) + update).astype(bf16)
-
-        if not last:
-            acc[...] = jnp.zeros_like(acc)
-
-            def step(i, carry):
-                block = fresh(i)
-                x[i] = block
-                acc[...] += self_dot(block)
-                return carry
-
-            lax.fori_loop(0, n, step, 0)
-        if first:
-            own.wait()
-            for k in order:
-                tsends[k].wait_recv()
-            for j, g in enumerate(others):
-                copy = remote(cols.at[grp], cols.at[grp], gss.at[j], grs.at[j], (g, row))
-                copy.start()
-                gsends.append(copy)
-        if last:
-            bsends = {}
-            for k in order:
-                to = lax.rem(row + k, n)
-                x[to] = fresh(to)
-                bsends[k] = remote(x.at[to], back.at[row], bss.at[k], brs.at[k], (grp, to))
-                bsends[k].start()
-            back[row] = fresh(row)
+    for j, g in enumerate(others):
+        gsends.append(remote(cols.at[grp], cols.at[grp], gss.at[j], grs.at[j], (g, row)))
+
+    recross.wait_recv()
+
+    def put_factor(i, j, value):
+        qh[block(i), block(j)], ql[block(i), block(j)] = split(value)
+
+    unpack(qin, put_factor)
+    for k in near_order:
+        at = lax.rem(seat + k, half)
+        afar[at] = apply(afar[at])
+        bsends[k] = remote(afar.at[at], back.at[mate], bss.at[k], brs.at[k], (grp, peer(k)))
+    back[mate] = apply(afar[seat])
+    cross.wait_send()
+    recross.wait_send()
     for k in order:
-        sends[k].wait_send()
         tsends[k].wait_send()
     for copy in gsends:
         copy.wait()
-    for k in order:
+    for k in near_order:
+        fsends[k].wait_send()
+        nsends[k].wait_send()
+        asends[k].wait()
         bsends[k].wait()
 
 
@@ -214,6 +335,7 @@
 
 VM = pl.BlockSpec(memory_space=pltpu.VMEM)
 SM = pl.BlockSpec(memory_space=pltpu.SMEM)
+ANY = pl.BlockSpec(memory_space=pl.ANY)
 
 
 def body(grad, weight, owner, tokens, counts):
@@ -223,34 +345,38 @@
     assert number == ranks
     ys = groups // CORES
     dma = pltpu.SemaphoreType.DMA
-    top = float(jnp.finfo(bf16).max)
-    raw = jnp.clip(grad, -top, top).astype(bf16)
-
     count = tokens.shape[0]
     share = count // groups
+    half = ranks // 2
     back, cols = pl.pallas_call(
         functools.partial(ortho_kernel, ranks, groups),
         out_shape=[
             jax.ShapeDtypeStruct((ranks, rows, width), bf16),
             jax.ShapeDtypeStruct((groups, ranks, share, rows), bf16),
         ],
-        in_specs=[VM, pl.BlockSpec(memory_space=pl.ANY)],
+        in_specs=[ANY, ANY],
         out_specs=[VM, VM],
         scratch_shapes=[
+            pltpu.VMEM((ranks, rows, width), f32),
             pltpu.VMEM((ranks, rows, width), bf16),
-            pltpu.VMEM((width, width), f32),
-            pltpu.VMEM((width, width), bf16),
-            pltpu.VMEM((width, width), bf16),
+            pltpu.VMEM((half, rows, width), bf16),
+            pltpu.VMEM((half, rows, width), bf16),
         ]
-        + [dma((ranks,))] * 4
+        + [pltpu.VMEM((width, width), f32)] * 2
+        + [pltpu.VMEM((packed_rows(width), TILE), f32)] * 4
+        + [pltpu.VMEM((width, width), bf16)] * 7
+        + [dma((ranks,))]
+        + [dma((half,))] * 4
+        + [dma] * 4
+        + [dma((half,))] * 4
+        + [dma((ranks,))] * 2
         + [dma((groups,))] * 2
-        + [dma((ranks,))] * 2
         + [dma],
         compiler_params=pltpu.CompilerParams(
             collective_id=0, has_side_effects=True, vmem_limit_bytes=48 * 1024 * 1024
         ),
         name="ortho",
-    )(raw, tokens)
+    )(grad, tokens)
     new_weight = (weight.astype(f32) - step_size * back.astype(f32)).astype(bf16)
 
     target = owner[:, 0]

time: 163 us -> 129 us (0.79)
  Pallas kernels: 154 us -> 121 us
  other arithmetic: 5.79 us -> 2.1 us
    pallas_call x1, Pallas kernels: 115 us -> 93.5 us  [body(): pl.pallas_call(functools.partial(ortho_kernel, ranks, groups), out_shape=...]
    pallas_call x1, Pallas kernels: 38.5 us -> 27.9 us  [body(): pl.pallas_call(functools.partial(project_kernel, ranks, groups), out_shap...]
    convert_element_type x1 -> x0, other arithmetic: 3.86 us -> none  [body(): raw = jnp.clip(grad, -top, top).astype(bf16)]
where the time goes in v1:
time: 129 us; the launch traced here: 128 us
  Pallas kernels  121 us (94%)
  local copies, waits for them, and re-layouts  3.44 us (3%)
  other arithmetic  2.1 us (2%)
  between operations  1.35 us (1%)
    pallas_call x1, Pallas kernels, body(): pl.pallas_call(functools.partial(ortho_kernel, ranks, groups), out_shape=...  93.5 us
    pallas_call x1, Pallas kernels, body(): pl.pallas_call(functools.partial(project_kernel, ranks, groups), out_shap...  27.9 us
    unnamed x12, local copies, waits for them, and re-layouts  3.26 us

profile of v1, /device:TPU:0, one launch (start us, length us, event | category | flops | bytes accessed | tf_op | source)
XLA Modules:
  0.0 128.4 jit_solution(9665993987037215965)
XLA Ops:
  0.6 0.0 copy-start.3
  0.6 1.4 %copy-done.3 = bf16[384,2048]{1,0:T(8,128)(2,1)S(1)} copy-done((bf16[384,2048]{1,0:T(8,128)(2,1)S(1)}, bf16[384,2048]{1,0:T(8,128)(2,1)}, u32[]{:S(2)}) %copy-start.3) | copy-done | bytes 1572888
  2.0 0.0 copy-start.4
  2.0 93.5 %ortho.1 = (bf16[8,256,512]{2,1,0:T(8,128)(2,1)S(1)}, bf16[4,8,96,256]{3,2,1,0:T(8,128)(2,1)S(1)}) custom-call(f32[8,256,512]{2,1,0:T(8,128)} %grad.1, bf16[384,2048]{1,0:T(8,128)(2,1)S(1)} %copy-done.3), custom_call_target="tpu_custom_call" | custom-call | tf_op jit(solution)/shard_map/ortho/pallas_call | solution.py:351
  95.6 0.0 copy-start.1
  95.6 0.0 copy-done.4
  95.6 0.0 copy-start.5
  95.6 0.8 subtract_convert_fusion.fresh
  96.5 0.4 copy-done.1
  96.9 0.0 copy-start
  96.9 0.0 copy-done.5
  96.9 0.2 convert_reduce_fusion
  97.1 0.1 fusion
  97.2 0.1 copy.8.index
  97.3 0.2 and_reduce_fusion
  97.5 0.1 copy.7
  97.6 0.0 copy-start.2
  97.6 1.4 %copy-done.2 = bf16[4,8,96,256]{3,2,1,0:T(8,128)(2,1)S(1)} copy-done((bf16[4,8,96,256]{3,2,1,0:T(8,128)(2,1)S(1)}, bf16[4,8,96,256]{3,2,1,0:T(8,128)(2,1)}, u32[]{:S(2)}) %copy-start.2) | copy-done | bytes 1572888
  99.0 27.9 %project.1 = bf16[384,128]{1,0:T(8,128)(2,1)S(1)} custom-call(s32[8,2]{1,0:T(8,128)S(1)} %copy.8.index, s32[8,2]{1,0:T(8,128)S(1)} %convert_element_type.20.valid, bf16[4,8,96,256]{3,2,1,0:T(8,128)(2,1)S(1)} %copy-done.2, bf16[8,256,512]{2,1,0:T(8,128)(2,1)S(1)} %subtract_convert_fusion.fresh), custom_call_target="tpu_custom_call" | custom-call | tf_op jit(solution)/shard_map/project/pallas_call | solution.py:393
  127.6 0.8 broadcast_select_fusion
  128.4 0.0 copy-done
  (4 shorter events, 0.0 us)
Async XLA Ops:
  0.6 1.4 %copy-start.3 = (bf16[384,2048]{1,0:T(8,128)(2,1)S(1)}, bf16[384,2048]{1,0:T(8,128)(2,1)}, u32[]{:S(2)}) copy-start(bf16[384,2048]{1,0:T(8,128)(2,1)} %tokens.1) | copy-start | bytes 4718596
  2.0 93.6 %copy-start.4 = (bf16[8,256,512]{2,1,0:T(8,128)(2,1)S(1)}, bf16[8,256,512]{2,1,0:T(8,128)(2,1)}, u32[]{:S(2)}) copy-start(bf16[8,256,512]{2,1,0:T(8,128)(2,1)} %param.6) | copy-start | bytes 6291460
  95.6 1.3 copy-start.1
  95.6 1.3 copy-start.5
  96.9 31.5 %copy-start = (bf16[8,256,512]{2,1,0:T(8,128)(2,1)}, bf16[8,256,512]{2,1,0:T(8,128)(2,1)S(1)}, u32[]{:S(2)}) copy-start(bf16[8,256,512]{2,1,0:T(8,128)(2,1)S(1)} %subtract_convert_fusion.fresh) | copy-start | bytes 6291460
  97.6 1.4 %copy-start.2 = (bf16[4,8,96,256]{3,2,1,0:T(8,128)(2,1)S(1)}, bf16[4,8,96,256]{3,2,1,0:T(8,128)(2,1)}, u32[]{:S(2)}) copy-start(bf16[4,8,96,256]{3,2,1,0:T(8,128)(2,1)} %copy-done.1) | copy-start | bytes 4718596

commit v2 on v1

--- a/solution.py
+++ b/solution.py
@@ -1,4 +1,5 @@
 import functools
+import math
 
 import jax
 import jax.numpy as jnp
@@ -8,10 +9,11 @@
 from jax.sharding import PartitionSpec as P
 
 ITERS = 5
-MOST = 2
 CORES = 2
-LAGS = (1, 3)
+LAGS = (1, 2, 3)
 TILE = 128
+PLANES = 4
+SPARE = 3 * 1024 * 1024
 
 coef_a = 3.4445
 coef_b = -4.775
@@ -105,10 +107,12 @@
         put(i + 1, i + 1, jnp.where(row > col, both, jnp.where(row < col, turned, diagonal)))
 
 
-def ortho_kernel(
-    n, groups, grad, tokens, back, cols, stage, raw, afar, near, acc, full, gout, gin, qout, qin,
-    gh, gl, ph, qh, ql, th, tl,
-    lsem, fss, frs, nss, nrs, css, crs, dss, drs, ass, ars, bss, brs, tss, trs, gss, grs, own_sem
+def step_kernel(
+    n, groups, counts, listed, grad, weight, tokens, back, mixed, cols, fresh, old,
+    stage, raw, afar, near, acc, full, gout, gin, qout, qin, gh, gl, ph, qh, ql, th, tl,
+    part, got1, gotx, goty, sum2, sum3, gotz,
+    lsem, fss, frs, nss, nrs, css, crs, dss, drs, ass, ars, bss, brs, tss, trs, gss, grs, own_sem, wsem, owner, osem,
+    ss1, rs1, ssx, rsx, ssy, rsy, ssz, rsz
 ):
     row, grp = lax.axis_index("row"), lax.axis_index("grp")
     others = [lax.rem(grp + k, groups) for k in range(1, groups)]
@@ -116,7 +120,6 @@
     order = far_first(n)
     half = n // 2
     side, seat = row // half, lax.rem(row, half)
-    mate = lax.rem(row + half, n)
     near_order = far_first(half)
     top = float(jnp.finfo(bf16).max)
 
@@ -127,7 +130,10 @@
         return lax.rem(seat + half - k, half)
 
     def across(r):
-        return lax.rem(r + half, n)
+        plane = n // PLANES
+        return n - plane - r + 2 * lax.rem(r, plane)
+
+    mate = across(row)
 
     def remote(src, dst, ss, rs, where):
         copy = pltpu.make_async_remote_copy(
@@ -162,6 +168,10 @@
         else:
             nsends[k] = remote(raw.at[slot], near.at[seat], nss.at[k], nrs.at[k], (grp, peer(k)))
 
+    fetch = pltpu.make_async_copy(weight, old, wsem)
+    fetch.start()
+    names = pltpu.make_async_copy(listed, owner, osem)
+    names.start()
     acc[...] = dot_t(afar[seat], afar[seat])
     for k in near_order:
         fsends[k].wait_recv()
@@ -169,6 +179,10 @@
     pack(acc, gout)
     cross = remote(gout, gin, css, crs, (grp, mate))
 
+    full[...] = dot_t(near[seat], near[seat])
+    for k in near_order:
+        nsends[k].wait_recv()
+        full[...] += dot_t(near[source(k)], near[source(k)])
     tsends = {}
     for k in order:
         to = lax.rem(row + k, n)
@@ -176,10 +190,6 @@
     own = pltpu.make_async_copy(share_of(row), cols.at[grp, row], own_sem)
     own.start()
 
-    full[...] = dot_t(near[seat], near[seat])
-    for k in near_order:
-        nsends[k].wait_recv()
-        full[...] += dot_t(near[source(k)], near[source(k)])
     cross.wait_recv()
 
     def put_sum(i, j, value):
@@ -243,99 +253,159 @@
         afar[at] = apply(afar[at])
         bsends[k] = remote(afar.at[at], back.at[mate], bss.at[k], brs.at[k], (grp, peer(k)))
     back[mate] = apply(afar[seat])
+    fetch.wait()
+    names.wait()
+
+    def renew(index):
+        fresh[index] = (old[index].astype(f32) - step_size * back[index].astype(f32)).astype(bf16)
+
+    renew(row)
+    for k in near_order:
+        asends[k].wait_recv()
+        renew(side * half + source(k))
+    renew(mate)
+    for copy in gsends:
+        copy.wait_recv()
+    for k in near_order:
+        bsends[k].wait_recv()
+        renew(across(side * half + source(k)))
+
+    project(
+        n, groups, remote, owner, counts, fresh, mixed, cols, part, got1, gotx, goty, sum2, sum3, gotz,
+        ss1, rs1, ssx, rsx, ssy, rsy, ssz, rsz
+    )
     cross.wait_send()
     recross.wait_send()
     for k in order:
         tsends[k].wait_send()
     for copy in gsends:
-        copy.wait()
+        copy.wait_send()
     for k in near_order:
         fsends[k].wait_send()
         nsends[k].wait_send()
-        asends[k].wait()
-        bsends[k].wait()
-
-
-def project_kernel(
-    n, groups, index, valid, cols, fresh, out, part, got1, sum1, got2, sum2, got3,
-    ss1, rs1, ss2, rs2, ss3, rs3
+        asends[k].wait_send()
+        bsends[k].wait_send()
+
+
+def project(
+    n, groups, remote, owner, counts, fresh, mixed, cols, part, got1, gotx, goty, sum2, sum3, gotz,
+    ss1, rs1, ssx, rsx, ssy, rsy, ssz, rsz
 ):
     row, grp = lax.axis_index("row"), lax.axis_index("grp")
-    ys = groups // CORES
+    lanes, ys = n // PLANES, groups // CORES
+    z, x = row // lanes, lax.rem(row, lanes)
     y, core = grp // CORES, lax.rem(grp, CORES)
-    count, piece = out.shape
-    partners = [y * CORES + (1 - core)]
-    partners += [lax.rem(y + j, ys) * CORES + core for j in range(1, ys)]
-    greet(n, groups, partners)
-    order = far_first(n) + [0]
-
-    def remote(src, dst, ss, rs, where):
-        copy = pltpu.make_async_remote_copy(
-            src_ref=src, dst_ref=dst, send_sem=ss, recv_sem=rs, device_id=where, device_id_type=MESH
-        )
-        copy.start()
-        return copy
-
-    one, two, three = {}, {}, {}
-
-    def stage1(k):
-        b = lax.rem(row + k, n)
-        tok = cols[:, b].reshape(count, cols.shape[3])
-        total = jnp.zeros((count, groups * piece), f32)
-        for s in range(MOST):
-            term = jnp.dot(tok, fresh[index[b, s]], preferred_element_type=f32)
-            total = total + jnp.where(valid[b, s] > 0, term, 0.0)
-        total = (total * groups ** (-0.5)).astype(bf16)
-        for g in range(groups):
-            part[k, g % CORES, g // CORES] = total[:, g * piece : (g + 1) * piece]
-        one[k] = remote(part.at[k, 1 - core], got1.at[k], ss1.at[k], rs1.at[k], (partners[0], row))
-
-    def stage2(k):
+    count, piece = mixed.shape
+    order = far_first(PLANES) + [0]
+    one, two, three, four = {}, {}, {}, {}
+
+    def matrices_of(b):
+        first, last = jnp.int32(n), jnp.int32(-1)
+        for e in range(n):
+            hit = owner[e] == b
+            first = jnp.minimum(first, jnp.where(hit, e, n))
+            last = jnp.maximum(last, jnp.where(hit, e, -1))
+        return first, last
+
+    def stage1(turn):
+        k = order[turn]
+        for j in range(lanes):
+            b = lax.rem(z + k, PLANES) * lanes + lax.rem(x + j, lanes)
+            first, last = matrices_of(b)
+            tok = cols[:, b].reshape(count, cols.shape[3])
+            total = jnp.where(last >= 0, dot(tok, fresh[jnp.minimum(first, n - 1)]), 0.0)
+            total = total + jnp.where(last > first, dot(tok, fresh[jnp.maximum(last, 0)]), 0.0)
+            total = (total * groups ** (-0.5)).astype(bf16)
+            for g in range(groups):
+                part[k, g % CORES, j, g // CORES] = total[:, g * piece : (g + 1) * piece]
+        one[k] = remote(part.at[k, 1 - core], got1.at[k], ss1.at[k], rs1.at[k], (y * CORES + 1 - core, row))
+
+    def to_x(k, j, src, dst):
+        where = (grp, z * lanes + lax.rem(x + j, lanes))
+        return remote(src, dst, ssx.at[k, j], rsx.at[k, j], where)
+
+    def to_y(k, j, src, dst):
+        where = (lax.rem(y + j, ys) * CORES + core, row)
+        return remote(src, dst, ssy.at[k, j], rsy.at[k, j], where)
+
+    def stage2(turn):
+        k = order[turn]
         one[k].wait_recv()
         two[k] = []
-        for j in range(1, ys):
-            to = lax.rem(y + j, ys)
-            both = part[k, core, to].astype(f32) + got1[k, to].astype(f32)
-            sum1[k, j] = both.astype(bf16)
-            two[k].append(
-                remote(sum1.at[k, j], got2.at[k, j], ss2.at[k, j], rs2.at[k, j], (partners[j], row))
-            )
-
-    def stage3(k):
-        total = part[k, core, y].astype(f32) + got1[k, y].astype(f32)
-        for j in range(1, ys):
-            two[k][j - 1].wait_recv()
-            total = total + got2[k, j].astype(f32)
+        for j in range(lanes):
+            for i in range(ys):
+                at = lax.rem(y + i, ys)
+                got1[k, j, at] = (part[k, core, j, at].astype(f32) + got1[k, j, at].astype(f32)).astype(bf16)
+        if turn % 2 == 0:
+            for j in range(1, lanes):
+                two[k].append(to_x(k, j, got1.at[k, j], gotx.at[k, j]))
+        else:
+            for i in range(1, ys):
+                two[k].append(to_y(k, i, got1.at[k, :, lax.rem(y + i, ys)], goty.at[k, i]))
+
+    def stage3(turn):
+        k = order[turn]
+        three[k] = []
+        for copy in two[k]:
+            copy.wait_recv()
+        if turn % 2 == 0:
+            for i in reversed(range(ys)):
+                at = lax.rem(y + i, ys)
+                total = got1[k, 0, at].astype(f32)
+                for j in range(1, lanes):
+                    total = total + gotx[k, j, at].astype(f32)
+                sum2[k, i] = total.astype(bf16)
+                if i:
+                    three[k].append(to_y(k, i, sum2.at[k, i], goty.at[k, i, 0]))
+        else:
+            for j in reversed(range(lanes)):
+                total = got1[k, j, y].astype(f32)
+                for i in range(1, ys):
+                    total = total + goty[k, i, j].astype(f32)
+                sum2[k, j] = total.astype(bf16)
+                if j:
+                    three[k].append(to_x(k, j, sum2.at[k, j], gotx.at[k, j, 0]))
+
+    def stage4(turn):
+        k = order[turn]
+        for copy in three[k]:
+            copy.wait_recv()
+        total = sum2[k, 0].astype(f32)
+        if turn % 2 == 0:
+            for i in range(1, ys):
+                total = total + goty[k, i, 0].astype(f32)
+        else:
+            for j in range(1, lanes):
+                total = total + gotx[k, j, 0].astype(f32)
         if k == 0:
             return total
-        sum2[k] = total.astype(bf16)
-        to = lax.rem(row + k, n)
-        three[k] = remote(sum2.at[k], got3.at[k], ss3.at[k], rs3.at[k], (grp, to))
+        sum3[k] = total.astype(bf16)
+        four[k] = remote(
+            sum3.at[k], gotz.at[k], ssz.at[k], rsz.at[k], (grp, lax.rem(z + k, PLANES) * lanes + x)
+        )
 
     final = None
-    lag2, lag3 = LAGS
-    for i in range(n + lag3):
-        if i < n:
-            stage1(order[i])
-        if lag2 <= i < n + lag2:
-            stage2(order[i - lag2])
-        if lag3 <= i < n + lag3:
-            final = stage3(order[i - lag3])
-    for k in reversed(order[:-1]):
-        three[k].wait_recv()
-        final = final + got3[k].astype(f32)
-    out[...] = final.astype(bf16)
+    for turn in range(PLANES + LAGS[2]):
+        if turn < PLANES:
+            stage1(turn)
+        for stage, lag in zip((stage2, stage3, stage4), LAGS):
+            if lag <= turn < PLANES + lag:
+                final = stage(turn - lag)
+    for k in order[:-1]:
+        four[k].wait_recv()
+        final = final + gotz[k].astype(f32)
+    live = lax.broadcasted_iota(jnp.int32, (count, piece), 0) < counts[0]
+    mixed[...] = jnp.where(live, final, 0.0).astype(bf16)
     for k in order:
-        one[k].wait_send()
-        for copy in two[k]:
+        for copy in [one[k]] + two[k] + three[k]:
             copy.wait_send()
         if k:
-            three[k].wait_send()
+            four[k].wait_send()
 
 
 VM = pl.BlockSpec(memory_space=pltpu.VMEM)
 SM = pl.BlockSpec(memory_space=pltpu.SMEM)
-ANY = pl.BlockSpec(memory_space=pl.ANY)
+HBM = pl.BlockSpec(memory_space=pltpu.HBM)
 
 
 def body(grad, weight, owner, tokens, counts):
@@ -343,80 +413,66 @@
     groups = lax.axis_size("grp")
     number, rows, width = grad.shape
     assert number == ranks
-    ys = groups // CORES
+    half = ranks // 2
+    lanes, ys = ranks // PLANES, groups // CORES
+    count = tokens.shape[0]
+    share, piece = count // groups, width // groups
     dma = pltpu.SemaphoreType.DMA
-    count = tokens.shape[0]
-    share = count // groups
-    half = ranks // 2
-    back, cols = pl.pallas_call(
-        functools.partial(ortho_kernel, ranks, groups),
+    vmem = pltpu.VMEM
+    packed = vmem((packed_rows(width), TILE), f32)
+    buffers = [
+        vmem((groups, ranks, share, rows), bf16),
+        vmem((ranks, rows, width), bf16),
+        vmem((ranks, rows, width), bf16),
+        vmem((ranks, rows, width), f32),
+        vmem((ranks, rows, width), bf16),
+        vmem((half, rows, width), bf16),
+        vmem((half, rows, width), bf16),
+    ]
+    buffers += [vmem((width, width), f32)] * 2
+    buffers += [packed] * 4
+    buffers += [vmem((width, width), bf16)] * 7
+    buffers += [
+        vmem((PLANES, CORES, lanes, ys, count, piece), bf16),
+        vmem((PLANES, lanes, ys, count, piece), bf16),
+        vmem((PLANES, lanes, ys, count, piece), bf16),
+        vmem((PLANES, ys, lanes, count, piece), bf16),
+        vmem((PLANES, max(ys, lanes), count, piece), bf16),
+        vmem((PLANES, count, piece), bf16),
+        vmem((PLANES, count, piece), bf16),
+    ]
+    semaphores = [dma((ranks,))]
+    semaphores += [dma((half,))] * 4
+    semaphores += [dma] * 4
+    semaphores += [dma((half,))] * 4
+    semaphores += [dma((ranks,))] * 2
+    semaphores += [dma((groups,))] * 2
+    semaphores += [dma] * 2
+    semaphores += [pltpu.SMEM((number,), jnp.int32), dma]
+    semaphores += [dma((PLANES,))] * 2
+    semaphores += [dma((PLANES, lanes))] * 2
+    semaphores += [dma((PLANES, ys))] * 2
+    semaphores += [dma((PLANES,))] * 2
+    lane = 128
+    held = sum(
+        math.prod(b.shape[:-1]) * pl.cdiv(b.shape[-1], lane) * lane * jnp.dtype(b.dtype).itemsize for b in buffers
+    )
+    back, mixed = pl.pallas_call(
+        functools.partial(step_kernel, ranks, groups),
         out_shape=[
             jax.ShapeDtypeStruct((ranks, rows, width), bf16),
-            jax.ShapeDtypeStruct((groups, ranks, share, rows), bf16),
+            jax.ShapeDtypeStruct((count, piece), bf16),
         ],
-        in_specs=[ANY, ANY],
+        in_specs=[SM, HBM, HBM, HBM, HBM],
         out_specs=[VM, VM],
-        scratch_shapes=[
-            pltpu.VMEM((ranks, rows, width), f32),
-            pltpu.VMEM((ranks, rows, width), bf16),
-            pltpu.VMEM((half, rows, width), bf16),
-            pltpu.VMEM((half, rows, width), bf16),
-        ]
-        + [pltpu.VMEM((width, width), f32)] * 2
-        + [pltpu.VMEM((packed_rows(width), TILE), f32)] * 4
-        + [pltpu.VMEM((width, width), bf16)] * 7
-        + [dma((ranks,))]
-        + [dma((half,))] * 4
-        + [dma] * 4
-        + [dma((half,))] * 4
-        + [dma((ranks,))] * 2
-        + [dma((groups,))] * 2
-        + [dma],
+        scratch_shapes=buffers + semaphores,
         compiler_params=pltpu.CompilerParams(
-            collective_id=0, has_side_effects=True, vmem_limit_bytes=48 * 1024 * 1024
+            collective_id=0, has_side_effects=True, vmem_limit_bytes=held + SPARE
         ),
-        name="ortho",
-    )(grad, tokens)
+        name="step",
+    )(counts, *[pltpu.with_memory_space_constraint(a, pltpu.HBM) for a in (owner[:, 0], grad, weight, tokens)])
     new_weight = (weight.astype(f32) - step_size * back.astype(f32)).astype(bf16)
-
-    target = owner[:, 0]
-    before = jnp.arange(number)[None, :] < jnp.arange(number)[:, None]
-    same = target[None, :] == target[:, None]
-    slot = jnp.sum((same & before).astype(jnp.int32), axis=1)
-    hit = (target[None, None, :] == jnp.arange(ranks)[:, None, None]) & (
-        slot[None, None, :] == jnp.arange(MOST)[None, :, None]
-    )
-    index = jnp.sum(hit * jnp.arange(number)[None, None, :], axis=2).astype(jnp.int32)
-    valid = jnp.any(hit, axis=2).astype(jnp.int32)
-
-    piece = width // groups
-    summed = pl.pallas_call(
-        functools.partial(project_kernel, ranks, groups),
-        out_shape=jax.ShapeDtypeStruct((count, piece), bf16),
-        in_specs=[SM, SM, VM, VM],
-        out_specs=VM,
-        scratch_shapes=[
-            pltpu.VMEM((ranks, CORES, ys, count, piece), bf16),
-            pltpu.VMEM((ranks, ys, count, piece), bf16),
-            pltpu.VMEM((ranks, ys, count, piece), bf16),
-            pltpu.VMEM((ranks, ys, count, piece), bf16),
-            pltpu.VMEM((ranks, count, piece), bf16),
-            pltpu.VMEM((ranks, count, piece), bf16),
-            dma((ranks,)),
-            dma((ranks,)),
-            dma((ranks, ys)),
-            dma((ranks, ys)),
-            dma((ranks,)),
-            dma((ranks,)),
-        ],
-        compiler_params=pltpu.CompilerParams(
-            collective_id=1, has_side_effects=True, vmem_limit_bytes=48 * 1024 * 1024
-        ),
-        name="project",
-    )(index, valid, cols, new_weight)
-    live = jnp.arange(count)[:, None] < counts[0]
-    mixed = jnp.where(live, summed, jnp.zeros_like(summed))
-    return (new_weight, mixed)
+    return new_weight, mixed
 
 
 def solution(mesh):

time: 129 us -> 121 us (0.938)
  Pallas kernels: 121 us -> 116 us
  local copies, waits for them, and re-layouts: 3.44 us -> 0.64 us
    pallas_call x2 -> x1, Pallas kernels: 121 us -> 116 us  [body(): pl.pallas_call(functools.partial(step_kernel, ranks, groups), out_shape=[...]
    unnamed x12 -> x3, local copies, waits for them, and re-layouts: 3.26 us -> 0.64 us
where the time goes in v2:
time: 121 us; the launch traced here: 120 us
  Pallas kernels  116 us (96%)
  other arithmetic  2.03 us (2%)
  between operations  1.3 us (1%)
    pallas_call x1, Pallas kernels, body(): pl.pallas_call(functools.partial(step_kernel, ranks, groups), out_shape=[...  116 us

profile of v2, /device:TPU:0, one launch (start us, length us, event | category | flops | bytes accessed | tf_op | source)
XLA Modules:
  0.0 120.4 jit_solution(8265744712136161140)
XLA Ops:
  1.3 0.0 copy-start
  1.3 116.4 %step.1 = (bf16[8,256,512]{2,1,0:T(8,128)(2,1)S(1)}, bf16[384,128]{1,0:T(8,128)(2,1)S(1)}) custom-call(s32[1]{0:T(128)S(6)} %copy.8.counts, s32[8]{0:T(128)} %bitcast.1, f32[8,256,512]{2,1,0:T(8,128)} %grad.1, bf16[8,256,512]{2,1,0:T(8,128)(2,1)} %weight.1, bf16[384,2048]{1,0:T(8,128)(2,1)} %tokens.1), custom_call_target="tpu_custom_call" | custom-call | tf_op jit(solution)/shard_map/step/pallas_call | solution.py:460
  117.7 0.0 copy-done
  117.7 2.0 %subtract_convert_fusion = bf16[8,256,512]{2,1,0:T(8,128)(2,1)} fusion(bf16[8,256,512]{2,1,0:T(8,128)(2,1)S(1)} %get-tuple-element.4, bf16[8,256,512]{2,1,0:T(8,128)(2,1)S(1)} %copy-done), kind=kLoop, calls=%fused_computation | loop fusion | flops 5242880 | bytes 6291456 | tf_op jit(solution)/shard_map/convert_element_type | solution.py:474
  119.7 0.6 copy.9
Async XLA Ops:
  1.3 116.4 %copy-start = (bf16[8,256,512]{2,1,0:T(8,128)(2,1)S(1)}, bf16[8,256,512]{2,1,0:T(8,128)(2,1)}, u32[]{:S(2)}) copy-start(bf16[8,256,512]{2,1,0:T(8,128)(2,1)} %weight.1) | copy-start | bytes 6291460

commit v3 on v2

--- a/solution.py
+++ b/solution.py
@@ -10,8 +10,9 @@
 
 ITERS = 5
 CORES = 2
-LAGS = (1, 2, 3)
+LAGS = (1, 3, 5)
 TILE = 128
+PAD = 16
 PLANES = 4
 SPARE = 3 * 1024 * 1024
 
@@ -65,63 +66,70 @@
 
 def packed_rows(width):
     count = width // TILE
-    return (count * (count - 1) // 2 + count // 2) * TILE + count // 2 * 8
+    return (count * (count - 1) // 2 + count // 2) * TILE + count // 2 * PAD
+
+
+def layout_of(width):
+    count = width // TILE
+    middle = count // 2
+    items, at, left = [], 0, 0
+    for low, high in ((0, middle), (middle, count)):
+        for i in range(low, high):
+            for j in range(i + 1, count):
+                items.append((at, i, j))
+                at += TILE
+        for i in range(low, high, 2):
+            items.append((at, i, i))
+            at += TILE + PAD
+        left = left or at
+    return items, left
 
 
 def pack(full, out):
-    count = full.shape[0] // TILE
     row, col = iotas(TILE)
-    at = 0
-    for i in range(count):
-        for j in range(i + 1, count):
-            out[at : at + TILE] = full[block(i), block(j)]
-            at += TILE
-    for i in range(0, count, 2):
+    for at, i, j in layout_of(full.shape[0])[0]:
+        if i < j:
+            out[at : at + TILE] = full[block(i), block(j)].astype(out.dtype)
+            continue
         one, two = full[block(i), block(i)], full[block(i + 1), block(i + 1)]
-        out[at : at + TILE] = jnp.where(row <= col, one, two)
-        at += TILE
+        out[at : at + TILE] = jnp.where(row <= col, one, two).astype(out.dtype)
         diagonal = jnp.sum(jnp.where(row == col, two, 0.0), axis=0, keepdims=True)
-        out[at : at + 8] = jnp.broadcast_to(diagonal, (8, TILE))
-        at += 8
-
-
-def unpack(packed, put):
-    count = 1
-    while packed_rows(count * TILE) < packed.shape[0]:
-        count += 1
+        out[at + TILE : at + TILE + PAD] = jnp.broadcast_to(diagonal, (PAD, TILE)).astype(out.dtype)
+
+
+def unpack(packed, width, put, low, high):
     row, col = iotas(TILE)
-    at = 0
-    for i in range(count):
-        for j in range(i + 1, count):
-            value = packed[at : at + TILE]
+    for at, i, j in layout_of(width)[0]:
+        if not low <= at < high:
+            continue
+        value = packed[at : at + TILE].astype(f32)
+        turned = value.T
+        if i < j:
             put(i, j, value)
-            put(j, i, value.T)
-            at += TILE
-    for i in range(0, count, 2):
-        both = packed[at : at + TILE]
-        turned = both.T
-        at += TILE
-        diagonal = jnp.broadcast_to(packed[at : at + 1], (TILE, TILE))
-        at += 8
-        put(i, i, jnp.where(row <= col, both, turned))
-        put(i + 1, i + 1, jnp.where(row > col, both, jnp.where(row < col, turned, diagonal)))
+            put(j, i, turned)
+            continue
+        diagonal = jnp.broadcast_to(packed[at + TILE : at + TILE + PAD].astype(f32)[:1], (TILE, TILE))
+        put(i, i, jnp.where(row <= col, value, turned))
+        put(i + 1, i + 1, jnp.where(row > col, value, jnp.where(row < col, turned, diagonal)))
 
 
 def step_kernel(
-    n, groups, counts, listed, grad, weight, tokens, back, mixed, cols, fresh, old,
-    stage, raw, afar, near, acc, full, gout, gin, qout, qin, gh, gl, ph, qh, ql, th, tl,
+    n, groups, counts, listed, grad, weight, tokens, fresh, mixed, cols, back, old,
+    stage, raw, afar, near, update, acc, full, gout, gin, gsum, qout, qin, dout, din, gh, gl, ph, qh, ql, th, tl,
     part, got1, gotx, goty, sum2, sum3, gotz,
-    lsem, fss, frs, nss, nrs, css, crs, dss, drs, ass, ars, bss, brs, tss, trs, gss, grs, own_sem, wsem, owner, osem,
+    lsem, fss, frs, nss, nrs, css, crs, dss, drs, ass, ars, bss, brs, tss, trs, gss, grs, own_sem, wsem, owner, osem, ess, ers,
     ss1, rs1, ssx, rsx, ssy, rsy, ssz, rsz
 ):
     row, grp = lax.axis_index("row"), lax.axis_index("grp")
     others = [lax.rem(grp + k, groups) for k in range(1, groups)]
-    greet(n, groups, others)
     order = far_first(n)
     half = n // 2
     side, seat = row // half, lax.rem(row, half)
     near_order = far_first(half)
     top = float(jnp.finfo(bf16).max)
+    width = acc.shape[0]
+    left = layout_of(width)[1]
+    pieces = ((0, left), (left, qout.shape[0]))
 
     def peer(k):
         return side * half + lax.rem(seat + k, half)
@@ -154,6 +162,7 @@
         load = pltpu.make_async_copy(grad.at[index], stage.at[slot], lsem.at[slot])
         load.start()
         loads.append((index, load))
+    greet(n, groups, others)
     fsends, nsends = {}, {}
     for slot, (k, helping) in enumerate(plan):
         index, load = loads[slot]
@@ -195,9 +204,9 @@
     def put_sum(i, j, value):
         acc[block(i), block(j)] = value
 
-    pack(full, qout)
-    qout[...] = qout[...] + gin[...]
-    unpack(qout, put_sum)
+    pack(full, gsum)
+    gsum[...] = gsum[...] + gin[...]
+    unpack(gsum, width, put_sum, 0, gsum.shape[0])
 
     total = acc[...]
     down, right = iotas(total.shape[0])
@@ -220,20 +229,27 @@
             th[...], tl[...] = split(coef_a * whole(gh, gl) + (dot(gh[...], ph[...]) + dot(gl[...], ph[...])))
             gh[...], gl[...] = split(coef_a * whole(th, tl) + (dot_t(ph[...], th[...]) + dot_t(ph[...], tl[...])))
         else:
-            full[...] = scale * factor
+            factor = scale * factor
+            diagonal = jnp.sum(jnp.where(eye, factor, 0.0), axis=0, keepdims=True)
+            dout[...] = jnp.broadcast_to(diagonal, dout.shape)
+            full[...] = jnp.where(eye, 0.0, factor)
     pack(full, qout)
-    recross = remote(qout, qin, dss, drs, (grp, mate))
-    qh[...], ql[...] = split(full[...])
-
-    def apply(value):
-        return (dot(value, qh[...]) + dot(value, ql[...])).astype(bf16)
+    outline = remote(dout, din, ess, ers, (grp, mate))
+    recross = []
+    for part_of, (low, high) in enumerate(pieces):
+        rows = pl.ds(low, high - low)
+        recross.append(remote(qout.at[rows], qin.at[rows], dss.at[part_of], drs.at[part_of], (grp, mate)))
+    qh[...] = full[...].astype(bf16)
+
+    def apply(value, columns, diagonal):
+        return (value[:, columns].astype(f32) * diagonal[:1, columns] + dot(value, qh[:, columns])).astype(bf16)
 
     asends, bsends = {}, {}
     for k in near_order:
         at = lax.rem(seat + k, half)
-        near[at] = apply(near[at])
+        near[at] = apply(near[at], slice(None), dout)
         asends[k] = remote(near.at[at], back.at[row], ass.at[k], ars.at[k], (grp, peer(k)))
-    back[row] = apply(near[seat])
+    back[row] = apply(near[seat], slice(None), dout)
 
     own.wait()
     for k in order:
@@ -242,17 +258,22 @@
     for j, g in enumerate(others):
         gsends.append(remote(cols.at[grp], cols.at[grp], gss.at[j], grs.at[j], (g, row)))
 
-    recross.wait_recv()
-
     def put_factor(i, j, value):
-        qh[block(i), block(j)], ql[block(i), block(j)] = split(value)
-
-    unpack(qin, put_factor)
-    for k in near_order:
-        at = lax.rem(seat + k, half)
-        afar[at] = apply(afar[at])
-        bsends[k] = remote(afar.at[at], back.at[mate], bss.at[k], brs.at[k], (grp, peer(k)))
-    back[mate] = apply(afar[seat])
+        qh[block(i), block(j)] = value.astype(bf16)
+
+    outline.wait_recv()
+    for part_of, (low, high) in enumerate(pieces):
+        recross[part_of].wait_recv()
+        unpack(qin, width, put_factor, low, high)
+        columns = slice(part_of * width // 2, (part_of + 1) * width // 2)
+        for k in near_order:
+            at = lax.rem(seat + k, half)
+            update[at, :, columns] = apply(afar[at], columns, din)
+            bsends[part_of, k] = remote(
+                update.at[at, :, columns], back.at[mate, :, columns],
+                bss.at[part_of, k], brs.at[part_of, k], (grp, peer(k))
+            )
+    back[mate] = apply(afar[seat], slice(None), din)
     fetch.wait()
     names.wait()
 
@@ -267,7 +288,8 @@
     for copy in gsends:
         copy.wait_recv()
     for k in near_order:
-        bsends[k].wait_recv()
+        bsends[0, k].wait_recv()
+        bsends[1, k].wait_recv()
         renew(across(side * half + source(k)))
 
     project(
@@ -275,7 +297,8 @@
         ss1, rs1, ssx, rsx, ssy, rsy, ssz, rsz
     )
     cross.wait_send()
-    recross.wait_send()
+    for copy in recross + [outline]:
+        copy.wait_send()
     for k in order:
         tsends[k].wait_send()
     for copy in gsends:
@@ -284,7 +307,8 @@
         fsends[k].wait_send()
         nsends[k].wait_send()
         asends[k].wait_send()
-        bsends[k].wait_send()
+        bsends[0, k].wait_send()
+        bsends[1, k].wait_send()
 
 
 def project(
@@ -403,6 +427,16 @@
             four[k].wait_send()
 
 
+def store_kernel(fresh, mixed, new_weight, out, fsem, msem):
+    copies = [pltpu.make_async_copy(mixed, out, msem)]
+    for i in range(fresh.shape[0]):
+        copies.append(pltpu.make_async_copy(fresh.at[i], new_weight.at[i], fsem.at[i]))
+    for copy in copies:
+        copy.start()
+    for copy in copies:
+        copy.wait()
+
+
 VM = pl.BlockSpec(memory_space=pltpu.VMEM)
 SM = pl.BlockSpec(memory_space=pltpu.SMEM)
 HBM = pl.BlockSpec(memory_space=pltpu.HBM)
@@ -428,9 +462,12 @@
         vmem((ranks, rows, width), bf16),
         vmem((half, rows, width), bf16),
         vmem((half, rows, width), bf16),
+        vmem((half, rows, width), bf16),
     ]
     buffers += [vmem((width, width), f32)] * 2
-    buffers += [packed] * 4
+    buffers += [packed] * 3
+    buffers += [vmem((packed_rows(width), TILE), bf16)] * 2
+    buffers += [vmem((8, width), f32)] * 2
     buffers += [vmem((width, width), bf16)] * 7
     buffers += [
         vmem((PLANES, CORES, lanes, ys, count, piece), bf16),
@@ -443,12 +480,15 @@
     ]
     semaphores = [dma((ranks,))]
     semaphores += [dma((half,))] * 4
-    semaphores += [dma] * 4
-    semaphores += [dma((half,))] * 4
+    semaphores += [dma] * 2
+    semaphores += [dma((2,))] * 2
+    semaphores += [dma((half,))] * 2
+    semaphores += [dma((2, half))] * 2
     semaphores += [dma((ranks,))] * 2
     semaphores += [dma((groups,))] * 2
     semaphores += [dma] * 2
     semaphores += [pltpu.SMEM((number,), jnp.int32), dma]
+    semaphores += [dma] * 2
     semaphores += [dma((PLANES,))] * 2
     semaphores += [dma((PLANES, lanes))] * 2
     semaphores += [dma((PLANES, ys))] * 2
@@ -457,7 +497,7 @@
     held = sum(
         math.prod(b.shape[:-1]) * pl.cdiv(b.shape[-1], lane) * lane * jnp.dtype(b.dtype).itemsize for b in buffers
     )
-    back, mixed = pl.pallas_call(
+    fresh, mixed = pl.pallas_call(
         functools.partial(step_kernel, ranks, groups),
         out_shape=[
             jax.ShapeDtypeStruct((ranks, rows, width), bf16),
@@ -471,8 +511,15 @@
         ),
         name="step",
     )(counts, *[pltpu.with_memory_space_constraint(a, pltpu.HBM) for a in (owner[:, 0], grad, weight, tokens)])
-    new_weight = (weight.astype(f32) - step_size * back.astype(f32)).astype(bf16)
-    return new_weight, mixed
+    return pl.pallas_call(
+        store_kernel,
+        out_shape=[jax.ShapeDtypeStruct(a.shape, bf16) for a in (fresh, mixed)],
+        in_specs=[VM, VM],
+        out_specs=[HBM, HBM],
+        scratch_shapes=[dma((ranks,)), dma],
+        compiler_params=pltpu.CompilerParams(vmem_limit_bytes=SPARE),
+        name="store",
+    )(fresh, mixed)
 
 
 def solution(mesh):

time: 121 us -> 109 us (0.901)
  Pallas kernels: 116 us -> 108 us
  other arithmetic: 2.03 us -> 0 us
    pallas_call x1, Pallas kernels: 116 us -> 106 us  [body(): pl.pallas_call(functools.partial(step_kernel, ranks, groups), out_shape=[...]
    convert_element_type x1 -> x0, other arithmetic: 2.03 us -> none  [body(): (weight.astype(f32) - step_size * back.astype(f32)).astype(bf16)]
    pallas_call x0 -> x1, Pallas kernels: none -> 1.42 us  [body(): pl.pallas_call(store_kernel, out_shape=[jax.ShapeDtypeStruct(a.shape, bf1...]
where the time goes in v3:
time: 109 us
  Pallas kernels  108 us (99%)
  between operations  1.45 us (1%)
    pallas_call x1, Pallas kernels, body(): pl.pallas_call(functools.partial(step_kernel, ranks, groups), out_shape=[...  106 us

profile of v3, /device:TPU:0, one launch (start us, length us, event | category | flops | bytes accessed | tf_op | source)
XLA Modules:
  0.0 109.0 jit_solution(4716741533186548174)
XLA Ops:
  1.3 106.1 %step.1 = (bf16[8,256,512]{2,1,0:T(8,128)(2,1)S(1)}, bf16[384,128]{1,0:T(8,128)(2,1)S(1)}) custom-call(s32[1]{0:T(128)S(6)} %copy.7.counts, s32[8]{0:T(128)} %bitcast.1, f32[8,256,512]{2,1,0:T(8,128)} %grad.1, bf16[8,256,512]{2,1,0:T(8,128)(2,1)} %weight.1, bf16[384,2048]{1,0:T(8,128)(2,1)} %tokens.1), custom_call_target="tpu_custom_call" | custom-call | tf_op jit(solution)/shard_map/step/pallas_call | solution.py:500
  107.4 1.4 %store.1 = (bf16[8,256,512]{2,1,0:T(8,128)(2,1)}, bf16[384,128]{1,0:T(8,128)(2,1)}) custom-call(bf16[8,256,512]{2,1,0:T(8,128)(2,1)S(1)} %get-tuple-element.4.fresh, bf16[384,128]{1,0:T(8,128)(2,1)S(1)} %get-tuple-element.5.mixed), custom_call_target="tpu_custom_call" | custom-call | tf_op jit(solution)/shard_map/store/pallas_call | solution.py:514

commit v4 on v3

--- a/solution.py
+++ b/solution.py
@@ -10,7 +10,7 @@
 
 ITERS = 5
 CORES = 2
-LAGS = (1, 3, 5)
+LAGS = (2, 4)
 TILE = 128
 PAD = 16
 PLANES = 4
@@ -116,16 +116,16 @@
 def step_kernel(
     n, groups, counts, listed, grad, weight, tokens, fresh, mixed, cols, back, old,
     stage, raw, afar, near, update, acc, full, gout, gin, gsum, qout, qin, dout, din, gh, gl, ph, qh, ql, th, tl,
-    part, got1, gotx, goty, sum2, sum3, gotz,
+    mine, theirs, given, got1, gotx, goty, sum2, sum3, gotz,
     lsem, fss, frs, nss, nrs, css, crs, dss, drs, ass, ars, bss, brs, tss, trs, gss, grs, own_sem, wsem, owner, osem, ess, ers,
-    ss1, rs1, ssx, rsx, ssy, rsy, ssz, rsz
+    theirs_of, oss, ors, hss, hrs, ssx, rsx, ssy, rsy, ssz, rsz
 ):
     row, grp = lax.axis_index("row"), lax.axis_index("grp")
     others = [lax.rem(grp + k, groups) for k in range(1, groups)]
     order = far_first(n)
     half = n // 2
     side, seat = row // half, lax.rem(row, half)
-    near_order = far_first(half)
+    near_order = list(range(1, half))
     top = float(jnp.finfo(bf16).max)
     width = acc.shape[0]
     left = layout_of(width)[1]
@@ -181,12 +181,16 @@
     fetch.start()
     names = pltpu.make_async_copy(listed, owner, osem)
     names.start()
+    naming = remote(listed, theirs_of, oss, ors, (grp + 1 - 2 * lax.rem(grp, CORES), row))
     acc[...] = dot_t(afar[seat], afar[seat])
     for k in near_order:
         fsends[k].wait_recv()
         acc[...] += dot_t(afar[source(k)], afar[source(k)])
     pack(acc, gout)
-    cross = remote(gout, gin, css, crs, (grp, mate))
+    cross = []
+    for part_of, (low, high) in enumerate(pieces):
+        rows = pl.ds(low, high - low)
+        cross.append(remote(gout.at[rows], gin.at[rows], css.at[part_of], crs.at[part_of], (grp, mate)))
 
     full[...] = dot_t(near[seat], near[seat])
     for k in near_order:
@@ -199,14 +203,15 @@
     own = pltpu.make_async_copy(share_of(row), cols.at[grp, row], own_sem)
     own.start()
 
-    cross.wait_recv()
+    pack(full, gsum)
 
     def put_sum(i, j, value):
         acc[block(i), block(j)] = value
 
-    pack(full, gsum)
-    gsum[...] = gsum[...] + gin[...]
-    unpack(gsum, width, put_sum, 0, gsum.shape[0])
+    for part_of, (low, high) in enumerate(pieces):
+        cross[part_of].wait_recv()
+        gsum[low:high] = gsum[low:high] + gin[low:high]
+        unpack(gsum, width, put_sum, low, high)
 
     total = acc[...]
     down, right = iotas(total.shape[0])
@@ -277,27 +282,43 @@
     fetch.wait()
     names.wait()
 
-    def renew(index):
-        fresh[index] = (old[index].astype(f32) - step_size * back[index].astype(f32)).astype(bf16)
-
-    renew(row)
+    twin = grp + 1 - 2 * lax.rem(grp, CORES)
+    first_core = lax.rem(grp, CORES) == 0
+    swaps = []
+
+    def renew(slot, index):
+        value = (old[index].astype(f32) - step_size * back[index].astype(f32)).astype(bf16)
+        fresh[index] = value
+        piece = width // groups
+        blocks = [value[:, g * piece : (g + 1) * piece] for g in range(groups)]
+        halves = [jnp.concatenate(blocks[c::CORES], axis=1) for c in range(CORES)]
+        mine[index] = jnp.where(first_core, halves[0], halves[1])
+        given[index] = jnp.where(first_core, halves[1], halves[0])
+        swaps.append(remote(given.at[index], theirs.at[index], hss.at[slot], hrs.at[slot], (twin, row)))
+
+    renew(0, row)
     for k in near_order:
         asends[k].wait_recv()
-        renew(side * half + source(k))
-    renew(mate)
+        renew(k, side * half + source(k))
+    renew(half, mate)
     for copy in gsends:
         copy.wait_recv()
     for k in near_order:
         bsends[0, k].wait_recv()
         bsends[1, k].wait_recv()
-        renew(across(side * half + source(k)))
-
+        renew(half + k, across(side * half + source(k)))
+
+    naming.wait_recv()
+    for copy in swaps:
+        copy.wait_recv()
     project(
-        n, groups, remote, owner, counts, fresh, mixed, cols, part, got1, gotx, goty, sum2, sum3, gotz,
-        ss1, rs1, ssx, rsx, ssy, rsy, ssz, rsz
+        n, groups, remote, (owner, theirs_of), counts, (mine, theirs), mixed, cols, got1, gotx, goty, sum2, sum3, gotz,
+        ssx, rsx, ssy, rsy, ssz, rsz
     )
-    cross.wait_send()
-    for copy in recross + [outline]:
+    naming.wait_send()
+    for copy in swaps:
+        copy.wait_send()
+    for copy in cross + recross + [outline]:
         copy.wait_send()
     for k in order:
         tsends[k].wait_send()
@@ -312,8 +333,8 @@
 
 
 def project(
-    n, groups, remote, owner, counts, fresh, mixed, cols, part, got1, gotx, goty, sum2, sum3, gotz,
-    ss1, rs1, ssx, rsx, ssy, rsy, ssz, rsz
+    n, groups, remote, owners, counts, weights, mixed, cols, got1, gotx, goty, sum2, sum3, gotz,
+    ssx, rsx, ssy, rsy, ssz, rsz
 ):
     row, grp = lax.axis_index("row"), lax.axis_index("grp")
     lanes, ys = n // PLANES, groups // CORES
@@ -321,9 +342,9 @@
     y, core = grp // CORES, lax.rem(grp, CORES)
     count, piece = mixed.shape
     order = far_first(PLANES) + [0]
-    one, two, three, four = {}, {}, {}, {}
-
-    def matrices_of(b):
+    two, three, four = {}, {}, {}
+
+    def matrices_of(owner, b):
         first, last = jnp.int32(n), jnp.int32(-1)
         for e in range(n):
             hit = owner[e] == b
@@ -331,19 +352,6 @@
             last = jnp.maximum(last, jnp.where(hit, e, -1))
         return first, last
 
-    def stage1(turn):
-        k = order[turn]
-        for j in range(lanes):
-            b = lax.rem(z + k, PLANES) * lanes + lax.rem(x + j, lanes)
-            first, last = matrices_of(b)
-            tok = cols[:, b].reshape(count, cols.shape[3])
-            total = jnp.where(last >= 0, dot(tok, fresh[jnp.minimum(first, n - 1)]), 0.0)
-            total = total + jnp.where(last > first, dot(tok, fresh[jnp.maximum(last, 0)]), 0.0)
-            total = (total * groups ** (-0.5)).astype(bf16)
-            for g in range(groups):
-                part[k, g % CORES, j, g // CORES] = total[:, g * piece : (g + 1) * piece]
-        one[k] = remote(part.at[k, 1 - core], got1.at[k], ss1.at[k], rs1.at[k], (y * CORES + 1 - core, row))
-
     def to_x(k, j, src, dst):
         where = (grp, z * lanes + lax.rem(x + j, lanes))
         return remote(src, dst, ssx.at[k, j], rsx.at[k, j], where)
@@ -352,15 +360,21 @@
         where = (lax.rem(y + j, ys) * CORES + core, row)
         return remote(src, dst, ssy.at[k, j], rsy.at[k, j], where)
 
-    def stage2(turn):
+    def stage1(turn):
         k = order[turn]
-        one[k].wait_recv()
         two[k] = []
         for j in range(lanes):
+            b = lax.rem(z + k, PLANES) * lanes + lax.rem(x + j, lanes)
+            tok = cols[:, b].reshape(count, cols.shape[3])
+            total = jnp.zeros((count, ys * piece), f32)
+            for owner, weight in zip(owners, weights):
+                first, last = matrices_of(owner, b)
+                total = total + jnp.where(last >= 0, dot(tok, weight[jnp.minimum(first, n - 1)]), 0.0)
+                total = total + jnp.where(last > first, dot(tok, weight[jnp.maximum(last, 0)]), 0.0)
+            total = (total * groups ** (-0.5)).astype(bf16)
             for i in range(ys):
-                at = lax.rem(y + i, ys)
-                got1[k, j, at] = (part[k, core, j, at].astype(f32) + got1[k, j, at].astype(f32)).astype(bf16)
-        if turn % 2 == 0:
+                got1[k, j, i] = total[:, i * piece : (i + 1) * piece]
+        if turn % 2 == 1:
             for j in range(1, lanes):
                 two[k].append(to_x(k, j, got1.at[k, j], gotx.at[k, j]))
         else:
@@ -372,7 +386,7 @@
         three[k] = []
         for copy in two[k]:
             copy.wait_recv()
-        if turn % 2 == 0:
+        if turn % 2 == 1:
             for i in reversed(range(ys)):
                 at = lax.rem(y + i, ys)
                 total = got1[k, 0, at].astype(f32)
@@ -395,7 +409,7 @@
         for copy in three[k]:
             copy.wait_recv()
         total = sum2[k, 0].astype(f32)
-        if turn % 2 == 0:
+        if turn % 2 == 1:
             for i in range(1, ys):
                 total = total + goty[k, i, 0].astype(f32)
         else:
@@ -409,10 +423,10 @@
         )
 
     final = None
-    for turn in range(PLANES + LAGS[2]):
+    for turn in range(PLANES + LAGS[1]):
         if turn < PLANES:
             stage1(turn)
-        for stage, lag in zip((stage2, stage3, stage4), LAGS):
+        for stage, lag in zip((stage3, stage4), LAGS):
             if lag <= turn < PLANES + lag:
                 final = stage(turn - lag)
     for k in order[:-1]:
@@ -421,7 +435,7 @@
     live = lax.broadcasted_iota(jnp.int32, (count, piece), 0) < counts[0]
     mixed[...] = jnp.where(live, final, 0.0).astype(bf16)
     for k in order:
-        for copy in [one[k]] + two[k] + three[k]:
+        for copy in two[k] + three[k]:
             copy.wait_send()
         if k:
             four[k].wait_send()
@@ -469,8 +483,8 @@
     buffers += [vmem((packed_rows(width), TILE), bf16)] * 2
     buffers += [vmem((8, width), f32)] * 2
     buffers += [vmem((width, width), bf16)] * 7
+    buffers += [vmem((ranks, rows, width // CORES), bf16)] * 3
     buffers += [
-        vmem((PLANES, CORES, lanes, ys, count, piece), bf16),
         vmem((PLANES, lanes, ys, count, piece), bf16),
         vmem((PLANES, lanes, ys, count, piece), bf16),
         vmem((PLANES, ys, lanes, count, piece), bf16),
@@ -480,8 +494,7 @@
     ]
     semaphores = [dma((ranks,))]
     semaphores += [dma((half,))] * 4
-    semaphores += [dma] * 2
-    semaphores += [dma((2,))] * 2
+    semaphores += [dma((2,))] * 4
     semaphores += [dma((half,))] * 2
     semaphores += [dma((2, half))] * 2
     semaphores += [dma((ranks,))] * 2
@@ -489,7 +502,8 @@
     semaphores += [dma] * 2
     semaphores += [pltpu.SMEM((number,), jnp.int32), dma]
     semaphores += [dma] * 2
-    semaphores += [dma((PLANES,))] * 2
+    semaphores += [pltpu.SMEM((number,), jnp.int32), dma, dma]
+    semaphores += [dma((ranks,))] * 2
     semaphores += [dma((PLANES, lanes))] * 2
     semaphores += [dma((PLANES, ys))] * 2
     semaphores += [dma((PLANES,))] * 2

time: 109 us -> 108 us (level)
  no operation moved by 1% of the time
where the time goes in v4:
time: 108 us
  Pallas kernels  107 us (99%)
  between operations  1.45 us (1%)
    pallas_call x1, Pallas kernels, body(): pl.pallas_call(functools.partial(step_kernel, ranks, groups), out_shape=[...  105 us

profile of v4, /device:TPU:0, one launch (start us, length us, event | category | flops | bytes accessed | tf_op | source)
XLA Modules:
  0.0 108.2 jit_solution(15516950374430744618)
XLA Ops:
  1.3 105.4 %step.1 = (bf16[8,256,512]{2,1,0:T(8,128)(2,1)S(1)}, bf16[384,128]{1,0:T(8,128)(2,1)S(1)}) custom-call(s32[1]{0:T(128)S(6)} %copy.7.counts, s32[8]{0:T(128)} %bitcast.1, f32[8,256,512]{2,1,0:T(8,128)} %grad.1, bf16[8,256,512]{2,1,0:T(8,128)(2,1)} %weight.1, bf16[384,2048]{1,0:T(8,128)(2,1)} %tokens.1), custom_call_target="tpu_custom_call" | custom-call | tf_op jit(solution)/shard_map/step/pallas_call | solution.py:514
  106.7 1.4 %store.1 = (bf16[8,256,512]{2,1,0:T(8,128)(2,1)}, bf16[384,128]{1,0:T(8,128)(2,1)}) custom-call(bf16[8,256,512]{2,1,0:T(8,128)(2,1)S(1)} %get-tuple-element.4.fresh, bf16[384,128]{1,0:T(8,128)(2,1)S(1)} %get-tuple-element.5.mixed), custom_call_target="tpu_custom_call" | custom-call | tf_op jit(solution)/shard_map/store/pallas_call | solution.py:528

commit v5 on v4

--- a/solution.py
+++ b/solution.py
@@ -308,11 +308,8 @@
         bsends[1, k].wait_recv()
         renew(half + k, across(side * half + source(k)))
 
-    naming.wait_recv()
-    for copy in swaps:
-        copy.wait_recv()
     project(
-        n, groups, remote, (owner, theirs_of), counts, (mine, theirs), mixed, cols, got1, gotx, goty, sum2, sum3, gotz,
+        n, groups, remote, [naming] + swaps, (owner, theirs_of), counts, (mine, theirs), mixed, cols, got1, gotx, goty, sum2, sum3, gotz,
         ssx, rsx, ssy, rsy, ssz, rsz
     )
     naming.wait_send()
@@ -333,7 +330,7 @@
 
 
 def project(
-    n, groups, remote, owners, counts, weights, mixed, cols, got1, gotx, goty, sum2, sum3, gotz,
+    n, groups, remote, arrivals, owners, counts, weights, mixed, cols, got1, gotx, goty, sum2, sum3, gotz,
     ssx, rsx, ssy, rsy, ssz, rsz
 ):
     row, grp = lax.axis_index("row"), lax.axis_index("grp")
@@ -363,14 +360,18 @@
     def stage1(turn):
         k = order[turn]
         two[k] = []
-        for j in range(lanes):
-            b = lax.rem(z + k, PLANES) * lanes + lax.rem(x + j, lanes)
-            tok = cols[:, b].reshape(count, cols.shape[3])
-            total = jnp.zeros((count, ys * piece), f32)
-            for owner, weight in zip(owners, weights):
+        totals = [jnp.zeros((count, ys * piece), f32)] * lanes
+        for source, (owner, weight) in enumerate(zip(owners, weights)):
+            if turn == 0 and source == 1:
+                for copy in arrivals:
+                    copy.wait_recv()
+            for j in range(lanes):
+                b = lax.rem(z + k, PLANES) * lanes + lax.rem(x + j, lanes)
+                tok = cols[:, b].reshape(count, cols.shape[3])
                 first, last = matrices_of(owner, b)
-                total = total + jnp.where(last >= 0, dot(tok, weight[jnp.minimum(first, n - 1)]), 0.0)
-                total = total + jnp.where(last > first, dot(tok, weight[jnp.maximum(last, 0)]), 0.0)
+                totals[j] = totals[j] + jnp.where(last >= 0, dot(tok, weight[jnp.minimum(first, n - 1)]), 0.0)
+                totals[j] = totals[j] + jnp.where(last > first, dot(tok, weight[jnp.maximum(last, 0)]), 0.0)
+        for j, total in enumerate(totals):
             total = (total * groups ** (-0.5)).astype(bf16)
             for i in range(ys):
                 got1[k, j, i] = total[:, i * piece : (i + 1) * piece]

time: 108 us -> 109 us (level)
  no operation moved by 1% of the time
where the time goes in v5:
time: 109 us
  Pallas kernels  108 us (99%)
  between operations  1.45 us (1%)
    pallas_call x1, Pallas kernels, body(): pl.pallas_call(functools.partial(step_kernel, ranks, groups), out_shape=[...  106 us

profile of v5, /device:TPU:0, one launch (start us, length us, event | category | flops | bytes accessed | tf_op | source)
XLA Modules:
  0.0 109.2 jit_solution(16203877088999634760)
XLA Ops:
  1.3 106.3 %step.1 = (bf16[8,256,512]{2,1,0:T(8,128)(2,1)S(1)}, bf16[384,128]{1,0:T(8,128)(2,1)S(1)}) custom-call(s32[1]{0:T(128)S(6)} %copy.7.counts, s32[8]{0:T(128)} %bitcast.1, f32[8,256,512]{2,1,0:T(8,128)} %grad.1, bf16[8,256,512]{2,1,0:T(8,128)(2,1)} %weight.1, bf16[384,2048]{1,0:T(8,128)(2,1)} %tokens.1), custom_call_target="tpu_custom_call" | custom-call | tf_op jit(solution)/shard_map/step/pallas_call | solution.py:515
  107.6 1.4 %store.1 = (bf16[8,256,512]{2,1,0:T(8,128)(2,1)}, bf16[384,128]{1,0:T(8,128)(2,1)}) custom-call(bf16[8,256,512]{2,1,0:T(8,128)(2,1)S(1)} %get-tuple-element.4.fresh, bf16[384,128]{1,0:T(8,128)(2,1)S(1)} %get-tuple-element.5.mixed), custom_call_target="tpu_custom_call" | custom-call | tf_op jit(solution)/shard_map/store/pallas_call | solution.py:529
